TPU v7x, 128 devices: a whole 4x4x4 slice. The times are simulated.
128 devices in a mesh: row: 8 (over z, x_hi), col: 16 (over y, x_lo, core).
Axes of the slice: x: 4 (x_hi: 2, x_lo: 2; x = x_hi * 2 + x_lo), y: 4, z: 4, core: 2. Of those that a mesh axis runs over, the one named last changes fastest.
Arguments:
- features: bfloat16 [32768, 512], P('row'), may hold values from -6 to 6
- logits: float32 [32768, 128], P(('row', 'col')), may hold values from -16 to 16
Outputs:
- memberships: float32 [32768, 128], P(('row', 'col'))
- standardized: float32 [32768, 128], P(('row', 'col'))
All inputs are finite; a program needn't handle non-finite values.
Results may differ from a plain program's by a relative error of at most 0.0003.
Values may be sent and summed in bfloat16 or wider, within the bound.
A program may use at most 64 MiB of HBM per device.

v0:
```python
import math
import jax
import jax.numpy as jnp
from jax import lax
from jax.sharding import PartitionSpec as P

ITERS = 2


def kernel_product(left_rows, right_rows, members):
    count = left_rows.shape[0]
    feature_width = left_rows.shape[1]
    block_rows = math.gcd(count, 512)
    blocks = left_rows.reshape(count // block_rows, block_rows, feature_width)

    def block_product(block):
        inner = jnp.einsum("bf,nf->bn", block, right_rows, preferred_element_type=jnp.float32)
        base = 1.0 + inner / feature_width
        kernel = base * base * base
        return jnp.dot(
            kernel, members, precision=lax.Precision.HIGHEST, preferred_element_type=jnp.float32
        )

    return lax.map(block_product, blocks).reshape(count, members.shape[1])


def on_device(features, logits):
    frames = logits.shape[0]
    column = lax.axis_index("col")
    own_rows = lax.dynamic_slice_in_dim(features, column * frames, frames, 0)
    column_panel = lax.all_gather(own_rows, "row", axis=0, tiled=True)
    raised = jnp.exp(logits)
    members = raised / jnp.sum(raised, axis=1, keepdims=True)
    standardized = members
    for iteration in range(ITERS):
        members_column = lax.all_gather(members, "row", axis=0, tiled=True)
        scores = lax.psum_scatter(
            kernel_product(features, column_panel, members_column),
            "col",
            scatter_dimension=0,
            tiled=True,
        )
        cluster_size, weighted = lax.psum(
            (jnp.sum(members, axis=0), jnp.sum(members * scores, axis=0)), ("row", "col")
        )
        compact = weighted / (cluster_size * cluster_size)
        distance = compact[None, :] - 2.0 * scores / cluster_size[None, :]
        centered = distance - jnp.mean(distance, axis=1, keepdims=True)
        spread = jnp.mean(centered * centered, axis=1, keepdims=True)
        standardized = centered / jnp.sqrt(spread + 1e-06)
        raised = jnp.exp(-2.0 * standardized)
        members = raised / jnp.sum(raised, axis=1, keepdims=True)
    return (members, standardized)


def solution(mesh):
    return jax.shard_map(
        on_device,
        mesh=mesh,
        in_specs=(P("row", None), P(("row", "col"), None)),
        out_specs=(P(("row", "col"), None), P(("row", "col"), None)),
        check_vma=False,
    )
```

profile of v0, /device:TPU:1, one launch (start us, length us, event | category | flops | bytes accessed | tf_op | source)
XLA Modules:
  0.0 545.2 jit_solution(2299477837792060629)
XLA Ops:
  11.7 47.2 %all-gather.6.cloned.1.call-done = f32[2048,128]{1,0:T(8,128)} async-done(((f32[256,128]{1,0:T(8,128)}), f32[2048,128]{1,0:T(8,128)}) %all-gather.6.cloned.1.call-update) | async-done | bytes 1048592 | tf_op jit(solution)/shard_map/all_gather | solution.py:36
  59.0 55.7 %all-gather.4.cloned.1.call-done = bf16[2048,512]{1,0:T(8,128)(2,1)} async-done(((bf16[256,512]{1,0:T(8,128)(2,1)}), bf16[2048,512]{1,0:T(8,128)(2,1)}) %all-gather.4.cloned.1.call-update) | async-done | bytes 2097168 | tf_op jit(solution)/shard_map/all_gather | solution.py:31
  114.8 54.8 %while.20 = (s32[]{:T(128)}, f32[8,512,128]{2,1,0:T(8,128)S(1)}, bf16[8,512,512]{2,1,0:T(8,128)(2,1)}, bf16[2048,512]{1,0:T(8,128)(2,1)}, f32[2048,128]{1,0:T(8,128)}, /*index=5*/s32[]{:T(128)}) while((s32[]{:T(128)}, f32[8,512,128]{2,1,0:T(8,128)S(1)}, bf16[8,512,512]{2,1,0:T(8,128)(2,1)}, bf16[2048,512]{1,0:T(8,128)(2,1)}, ...), condition=%wide.region_2.3_spmd, body=%wide.region_1.2_spmd.sunk | while | flops 2688548864 | bytes 16515685 | solution.py:24
  114.9 3.1 fusion.48
  118.0 3.7 fusion.49
  121.7 3.1 fusion.48
  124.9 3.7 fusion.49
  128.6 3.1 fusion.48
  131.7 3.7 fusion.49
  138.6 3.7 fusion.49
  145.4 3.7 fusion.49
  152.3 3.7 fusion.49
  156.0 3.1 fusion.48
  159.1 3.7 fusion.49
  166.0 3.7 fusion.49
  171.0 60.5 %reduce-scatter.3.cloned.1.call-done = f32[256,128]{1,0:T(8,128)} async-done(((f32[4096,128]{1,0:T(8,128)}), f32[256,128]{1,0:T(8,128)}) %reduce-scatter.3.cloned.1.call-update) | async-done | bytes 131088 | tf_op jit(solution)/shard_map/reduce_scatter | solution.py:37
  232.5 68.0 %all-reduce.1 = (f32[128]{0:T(128)S(1)}, f32[128]{0:T(128)S(1)}) all-reduce(f32[128]{0:T(128)S(1)} %get-tuple-element.61, f32[128]{0:T(128)S(1)} %get-tuple-element.60), channel_id=1, replica_groups=mesh['row'=8,'col'=16] {'row','col'}, use_global_device_ids=true, to_apply=%region_7.8 | all-reduce | flops 256 | bytes 2048 | tf_op jit(solution)/shard_map/psum | solution.py:43
  305.8 41.2 %all-gather.8.cloned.1.call-done = f32[2048,128]{1,0:T(8,128)} async-done(((f32[256,128]{1,0:T(8,128)}), f32[2048,128]{1,0:T(8,128)}) %all-gather.8.cloned.1.call-update) | async-done | bytes 1048592 | tf_op jit(solution)/shard_map/all_gather | solution.py:36
  347.2 54.8 %while.21 = (s32[]{:T(128)}, f32[8,512,128]{2,1,0:T(8,128)S(1)}, bf16[8,512,512]{2,1,0:T(8,128)(2,1)}, bf16[2048,512]{1,0:T(8,128)(2,1)}, f32[2048,128]{1,0:T(8,128)}, /*index=5*/s32[]{:T(128)}) while((s32[]{:T(128)}, f32[8,512,128]{2,1,0:T(8,128)S(1)}, bf16[8,512,512]{2,1,0:T(8,128)(2,1)}, bf16[2048,512]{1,0:T(8,128)(2,1)}, ...), condition=%wide.region_12.13_spmd, body=%wide.region_11.12_spmd.sunk | while | flops 2688548864 | bytes 16515685 | solution.py:24
  347.2 3.1 fusion.53
  350.3 3.7 fusion.54
  354.1 3.1 fusion.53
  357.2 3.7 fusion.54
  364.1 3.7 fusion.54
  370.9 3.7 fusion.54
  377.8 3.7 fusion.54
  381.5 3.1 fusion.53
  384.6 3.7 fusion.54
  391.5 3.7 fusion.54
  398.3 3.7 fusion.54
  403.4 62.6 %reduce-scatter.5.cloned.1.call-done = f32[256,128]{1,0:T(8,128)} async-done(((f32[4096,128]{1,0:T(8,128)}), f32[256,128]{1,0:T(8,128)}) %reduce-scatter.5.cloned.1.call-update) | async-done | bytes 131088 | tf_op jit(solution)/shard_map/reduce_scatter | solution.py:37
  467.1 67.5 %all-reduce = (f32[128]{0:T(128)S(1)}, f32[128]{0:T(128)S(1)}) all-reduce(f32[128]{0:T(128)S(1)} %get-tuple-element.59, f32[128]{0:T(128)S(1)} %get-tuple-element.58), channel_id=1, replica_groups=mesh['row'=8,'col'=16] {'row','col'}, use_global_device_ids=true, to_apply=%region_17.18 | all-reduce | flops 256 | bytes 2048 | tf_op jit(solution)/shard_map/psum | solution.py:43
  (82 shorter events, 47.0 us)
Async XLA Ops:
  7.2 51.8 %all-gather.6.cloned.1.call-start = ((), (), s32[]{:S(2)}) async-start(), calls=%async_computation.3 | async-start | bytes 1179648 | tf_op jit(solution)/shard_map/all_gather | solution.py:36
  9.9 104.8 %all-gather.4.cloned.1.call-start = ((), (), s32[]{:S(2)}) async-start(), calls=%async_computation.2 | async-start | bytes 2359296 | tf_op jit(solution)/shard_map/all_gather | solution.py:31
  11.7 219.8 %reduce-scatter.3.cloned.1.call-start = ((), (), s32[]{:S(2)}) async-start(), calls=%async_computation.4 | async-start | bytes 2228224 | tf_op jit(solution)/shard_map/reduce_scatter | solution.py:37
  114.8 116.7 %copy-start.3 = (f32[256,128]{1,0:T(8,128)S(1)}, f32[256,128]{1,0:T(8,128)}, u32[]{:S(2)}) copy-start(f32[256,128]{1,0:T(8,128)} %param.7) | copy-start | bytes 393220
  114.8 3.1 copy-start.5
  121.7 3.1 copy-start.5
  128.6 3.1 copy-start.5
  135.4 3.1 copy-start.5
  142.3 3.1 copy-start.5
  149.1 3.1 copy-start.5
  156.0 3.1 copy-start.5
  162.8 3.1 copy-start.5
  169.7 1.3 copy-start.1
  171.0 176.0 %all-gather.8.cloned.1.call-start = ((), (), s32[]{:S(2)}) async-start(), calls=%async_computation.5 | async-start | bytes 1179648 | tf_op jit(solution)/shard_map/all_gather | solution.py:36
  305.6 160.4 %reduce-scatter.5.cloned.1.call-start = ((), (), s32[]{:S(2)}) async-start(), calls=%async_computation.6 | async-start | bytes 2228224 | tf_op jit(solution)/shard_map/reduce_scatter | solution.py:37
  347.2 118.8 %copy-start.2 = (f32[256,128]{1,0:T(8,128)S(1)}, f32[256,128]{1,0:T(8,128)}, u32[]{:S(2)}) copy-start(f32[256,128]{1,0:T(8,128)} %reduce-scatter.3.cloned.1.call-done) | copy-start | bytes 393220
  347.2 3.1 copy-start.6
  354.1 3.1 copy-start.6
  360.9 3.1 copy-start.6
  367.8 3.1 copy-start.6
  374.6 3.1 copy-start.6
  381.5 3.1 copy-start.6
  388.3 3.1 copy-start.6
  395.2 3.1 copy-start.6
  402.0 1.4 copy-start
  537.9 0.8 copy-start.4
Sparse Core Ops, SparseCore 0:
  10.9 48.0 all-gather.5
  61.3 53.3 all-gather.3
  171.1 60.3 reduce-scatter.2
  305.7 41.2 all-gather.7
  403.5 62.4 reduce-scatter.4
where the time goes:
time: 546 us; the launch traced here: 545 us
  waiting for transfers between devices  267 us (49%)
  blocking collectives  136 us (25%)
  matrix products  109 us (20%)
  between operations  13.9 us (3%)
  other arithmetic  13.8 us (3%)
    psum x2, blocking collectives, on_device(): lax.psum((jnp.sum(members, axis=0), jnp.sum(members * scores, axis=0)), (...  136 us
    reduce_scatter x2, waiting for transfers between devices, on_device(): lax.psum_scatter(kernel_product(features, column_panel, members_column),...  123 us
    all_gather x2, waiting for transfers between devices, on_device(): members_column = lax.all_gather(members, 'row', axis=0, tiled=True)  88.4 us
    dot_general x16, matrix products, block_product(): jnp.dot(kernel, members, precision=lax.Precision.HIGHEST, preferred_eleme...  58.9 us
    all_gather x1, waiting for transfers between devices, on_device(): column_panel = lax.all_gather(own_rows, 'row', axis=0, tiled=True)  55.7 us
    dot_general x16, matrix products, block_product(): jnp.einsum('bf,nf->bn', block, right_rows, preferred_element_type=jnp.flo...  50 us
  transfers between devices with their start and end apart: 5, of which 5 were waited for; matrix products, arithmetic and copies ran while one was open for 0% of the time, Pallas kernels for 0%

commit v1 on v0

--- a/solution.py
+++ b/solution.py
@@ -28,7 +28,9 @@
     frames = logits.shape[0]
     column = lax.axis_index("col")
     own_rows = lax.dynamic_slice_in_dim(features, column * frames, frames, 0)
-    column_panel = lax.all_gather(own_rows, "row", axis=0, tiled=True)
+    column_panel = jnp.concatenate(
+        lax.all_to_all(jnp.stack([own_rows] * lax.axis_size("row")), "row", 0, 0), axis=0
+    )
     raised = jnp.exp(logits)
     members = raised / jnp.sum(raised, axis=1, keepdims=True)
     standardized = members

time: 546 us -> 505 us (0.925)
  waiting for transfers between devices: 267 us -> 220 us
  starting transfers between devices: 0.39 us -> 8.65 us
    all_gather x1 -> x0, waiting for transfers between devices: 55.7 us -> none  [on_device(): column_panel = lax.all_gather(own_rows, 'row', axis=0, tiled=True)]
    all_to_all x0 -> x1, waiting for transfers between devices: none -> 28 us  [on_device(): lax.all_to_all(jnp.stack([own_rows] * lax.axis_size('row')), 'row', 0, 0)]
    all_gather x2, waiting for transfers between devices: 88.4 us -> 66.9 us  [on_device(): members_column = lax.all_gather(members, 'row', axis=0, tiled=True)]
    all_to_all x0 -> x1, starting transfers between devices: none -> 8.31 us  [on_device(): lax.all_to_all(jnp.stack([own_rows] * lax.axis_size('row')), 'row', 0, 0)]
where the time goes in v1:
time: 505 us
  waiting for transfers between devices  220 us (44%)
  blocking collectives  135 us (27%)
  matrix products  109 us (22%)
  between operations  13.9 us (3%)
  other arithmetic  12 us (2%)
  starting transfers between devices  8.65 us (2%)
  local copies, waits for them, and re-layouts  5.53 us (1%)
    psum x2, blocking collectives, on_device(): lax.psum((jnp.sum(members, axis=0), jnp.sum(members * scores, axis=0)), (...  135 us
    reduce_scatter x2, waiting for transfers between devices, on_device(): lax.psum_scatter(kernel_product(features, column_panel, members_column),...  125 us
    all_gather x2, waiting for transfers between devices, on_device(): members_column = lax.all_gather(members, 'row', axis=0, tiled=True)  66.9 us
    dot_general x16, matrix products, block_product(): jnp.dot(kernel, members, precision=lax.Precision.HIGHEST, preferred_eleme...  58.9 us
    dot_general x16, matrix products, block_product(): jnp.einsum('bf,nf->bn', block, right_rows, preferred_element_type=jnp.flo...  50 us
    all_to_all x1, waiting for transfers between devices, on_device(): lax.all_to_all(jnp.stack([own_rows] * lax.axis_size('row')), 'row', 0, 0)  28 us
  transfers between devices with their start and end apart: 5, of which 5 were waited for; matrix products, arithmetic and copies ran while one was open for 0% of the time, Pallas kernels for 0%

profile of v1, /device:TPU:1, one launch (start us, length us, event | category | flops | bytes accessed | tf_op | source)
XLA Modules:
  0.0 505.0 jit_solution(4477725217365583627)
XLA Ops:
  9.7 8.3 %all-to-all-start = ((bf16[8,256,512]{2,1,0:T(8,128)(2,1)}), bf16[8,256,512]{2,1,0:T(8,128)(2,1)S(1)}, u32[]{:S(2)}, u32[]{:S(2)}) async-start(bf16[8,256,512]{2,1,0:T(8,128)(2,1)} %stack.2), calls=%async_computation | async-start | bytes 4194304 | tf_op jit(solution)/shard_map/all_to_all | solution.py:32
  19.0 28.0 %all-to-all-done = bf16[8,256,512]{2,1,0:T(8,128)(2,1)S(1)} async-done(((bf16[8,256,512]{2,1,0:T(8,128)(2,1)}), bf16[8,256,512]{2,1,0:T(8,128)(2,1)S(1)}, u32[]{:S(2)}, u32[]{:S(2)}) %all-to-all-start) | async-done | bytes 2097184 | tf_op jit(solution)/shard_map/all_to_all | solution.py:32
  47.0 25.8 %all-gather.3.cloned.1.call-done = f32[2048,128]{1,0:T(8,128)} async-done(((f32[256,128]{1,0:T(8,128)}), f32[2048,128]{1,0:T(8,128)}) %all-gather.3.cloned.1.call-update) | async-done | bytes 1048592 | tf_op jit(solution)/shard_map/all_gather | solution.py:38
  73.0 54.8 %while.20 = (s32[]{:T(128)}, f32[8,512,128]{2,1,0:T(8,128)S(1)}, bf16[8,512,512]{2,1,0:T(8,128)(2,1)}, bf16[2048,512]{1,0:T(8,128)(2,1)}, f32[2048,128]{1,0:T(8,128)}, /*index=5*/s32[]{:T(128)}) while((s32[]{:T(128)}, f32[8,512,128]{2,1,0:T(8,128)S(1)}, bf16[8,512,512]{2,1,0:T(8,128)(2,1)}, bf16[2048,512]{1,0:T(8,128)(2,1)}, ...), condition=%wide.region_2.3_spmd, body=%wide.region_1.2_spmd.sunk | while | flops 2688548864 | bytes 16515685 | solution.py:24
  73.0 3.1 fusion.48
  76.2 3.7 fusion.49
  79.9 3.1 fusion.48
  83.0 3.7 fusion.49
  86.7 3.1 fusion.48
  89.9 3.7 fusion.49
  96.7 3.7 fusion.49
  103.6 3.7 fusion.49
  110.4 3.7 fusion.49
  114.1 3.1 fusion.48
  117.3 3.7 fusion.49
  124.1 3.7 fusion.49
  129.2 62.5 %reduce-scatter.3.cloned.1.call-done = f32[256,128]{1,0:T(8,128)} async-done(((f32[4096,128]{1,0:T(8,128)}), f32[256,128]{1,0:T(8,128)}) %reduce-scatter.3.cloned.1.call-update) | async-done | bytes 131088 | tf_op jit(solution)/shard_map/reduce_scatter | solution.py:39
  192.8 67.7 %all-reduce.1 = (f32[128]{0:T(128)S(1)}, f32[128]{0:T(128)S(1)}) all-reduce(f32[128]{0:T(128)S(1)} %get-tuple-element.61, f32[128]{0:T(128)S(1)} %get-tuple-element.60), channel_id=1, replica_groups=mesh['row'=8,'col'=16] {'row','col'}, use_global_device_ids=true, to_apply=%region_7.8 | all-reduce | flops 256 | bytes 2048 | tf_op jit(solution)/shard_map/psum | solution.py:45
  265.7 41.1 %all-gather.5.cloned.1.call-done = f32[2048,128]{1,0:T(8,128)} async-done(((f32[256,128]{1,0:T(8,128)}), f32[2048,128]{1,0:T(8,128)}) %all-gather.5.cloned.1.call-update) | async-done | bytes 1048592 | tf_op jit(solution)/shard_map/all_gather | solution.py:38
  307.0 54.8 %while.21 = (s32[]{:T(128)}, f32[8,512,128]{2,1,0:T(8,128)S(1)}, bf16[8,512,512]{2,1,0:T(8,128)(2,1)}, bf16[2048,512]{1,0:T(8,128)(2,1)}, f32[2048,128]{1,0:T(8,128)}, /*index=5*/s32[]{:T(128)}) while((s32[]{:T(128)}, f32[8,512,128]{2,1,0:T(8,128)S(1)}, bf16[8,512,512]{2,1,0:T(8,128)(2,1)}, bf16[2048,512]{1,0:T(8,128)(2,1)}, ...), condition=%wide.region_12.13_spmd, body=%wide.region_11.12_spmd.sunk | while | flops 2688548864 | bytes 16515685 | solution.py:24
  307.0 3.1 fusion.53
  310.1 3.7 fusion.54
  317.0 3.7 fusion.54
  323.8 3.7 fusion.54
  330.7 3.7 fusion.54
  334.4 3.1 fusion.53
  337.5 3.7 fusion.54
  344.4 3.7 fusion.54
  351.2 3.7 fusion.54
  358.1 3.7 fusion.54
  363.2 62.5 %reduce-scatter.5.cloned.1.call-done = f32[256,128]{1,0:T(8,128)} async-done(((f32[4096,128]{1,0:T(8,128)}), f32[256,128]{1,0:T(8,128)}) %reduce-scatter.5.cloned.1.call-update) | async-done | bytes 131088 | tf_op jit(solution)/shard_map/reduce_scatter | solution.py:39
  426.8 67.7 %all-reduce = (f32[128]{0:T(128)S(1)}, f32[128]{0:T(128)S(1)}) all-reduce(f32[128]{0:T(128)S(1)} %get-tuple-element.59, f32[128]{0:T(128)S(1)} %get-tuple-element.58), channel_id=1, replica_groups=mesh['row'=8,'col'=16] {'row','col'}, use_global_device_ids=true, to_apply=%region_17.18 | all-reduce | flops 256 | bytes 2048 | tf_op jit(solution)/shard_map/psum | solution.py:45
  (84 shorter events, 49.1 us)
Async XLA Ops:
  7.2 10.9 %copy-start.4 = (f32[256,128]{1,0:T(8,128)S(1)}, f32[256,128]{1,0:T(8,128)}, u32[]{:S(2)}) copy-start(f32[256,128]{1,0:T(8,128)} %param.7) | copy-start | bytes 393220
  9.7 37.3 %all-to-all-start = ((bf16[8,256,512]{2,1,0:T(8,128)(2,1)}), bf16[8,256,512]{2,1,0:T(8,128)(2,1)S(1)}, u32[]{:S(2)}, u32[]{:S(2)}) async-start(bf16[8,256,512]{2,1,0:T(8,128)(2,1)} %stack.2), calls=%async_computation | async-start | bytes 4194304 | tf_op jit(solution)/shard_map/all_to_all | solution.py:32
  18.0 54.8 %all-gather.3.cloned.1.call-start = ((), (), s32[]{:S(2)}) async-start(), calls=%async_computation.3 | async-start | bytes 1179648 | tf_op jit(solution)/shard_map/all_gather | solution.py:38
  19.0 172.7 %reduce-scatter.3.cloned.1.call-start = ((), (), s32[]{:S(2)}) async-start(), calls=%async_computation.4 | async-start | bytes 2228224 | tf_op jit(solution)/shard_map/reduce_scatter | solution.py:39
  47.0 25.8 %copy-start.3 = (bf16[8,256,512]{2,1,0:T(8,128)(2,1)}, bf16[8,256,512]{2,1,0:T(8,128)(2,1)S(1)}, u32[]{:S(2)}) copy-start(bf16[8,256,512]{2,1,0:T(8,128)(2,1)S(1)} %all-to-all-done) | copy-start | bytes 6291460
  73.0 3.1 copy-start.6
  79.9 3.1 copy-start.6
  86.7 3.1 copy-start.6
  93.6 3.1 copy-start.6
  100.4 3.1 copy-start.6
  107.3 3.1 copy-start.6
  114.1 3.1 copy-start.6
  121.0 3.1 copy-start.6
  127.8 1.3 copy-start.1
  129.1 177.7 %all-gather.5.cloned.1.call-start = ((), (), s32[]{:S(2)}) async-start(), calls=%async_computation.5 | async-start | bytes 1179648 | tf_op jit(solution)/shard_map/all_gather | solution.py:38
  265.5 160.2 %reduce-scatter.5.cloned.1.call-start = ((), (), s32[]{:S(2)}) async-start(), calls=%async_computation.6 | async-start | bytes 2228224 | tf_op jit(solution)/shard_map/reduce_scatter | solution.py:39
  307.0 118.7 %copy-start.2 = (f32[256,128]{1,0:T(8,128)S(1)}, f32[256,128]{1,0:T(8,128)}, u32[]{:S(2)}) copy-start(f32[256,128]{1,0:T(8,128)} %reduce-scatter.3.cloned.1.call-done) | copy-start | bytes 393220
  307.0 3.1 copy-start.7
  313.8 3.1 copy-start.7
  320.7 3.1 copy-start.7
  327.5 3.1 copy-start.7
  334.4 3.1 copy-start.7
  341.3 3.1 copy-start.7
  348.1 3.1 copy-start.7
  355.0 3.1 copy-start.7
  361.8 1.4 copy-start
  497.7 0.8 copy-start.5
Sparse Core Ops, SparseCore 0:
  21.8 51.0 all-gather.2
  129.3 62.4 reduce-scatter.2
  265.6 41.1 all-gather.4
  363.3 62.3 reduce-scatter.4
